TPU v7x, 128 devices: a whole 4x4x4 slice. The times are simulated.
128 devices in a mesh: row: 16 (over z_lo, y, core), col: 8 (over x, z_hi).
Axes of the slice: x: 4, y: 4, z: 4 (z_hi: 2, z_lo: 2; z = z_hi * 2 + z_lo), core: 2. Of those that a mesh axis runs over, the one named last changes fastest.
Arguments:
- pair: bfloat16 [1024, 1024, 128], P('row', 'col'), may hold values from -6 to 6
- ln_gain: float32 [128], replicated, may hold values from 0.1 to 1.9
- ln_bias: float32 [128], replicated, may hold values from -3 to 3
- gate_weight: bfloat16 [128, 512], replicated, may hold values from -0.5 to 0.5
- up_weight: bfloat16 [128, 512], replicated, may hold values from -0.5 to 0.5
- out_weight: bfloat16 [512, 128], replicated, may hold values from -0.25 to 0.25
- head_weight: bfloat16 [128, 64], replicated, may hold values from -1 to 1
- targets: int32 [1024, 1024], P(('row', 'col')), may hold values from 0 to 63
- pair_mask: int32 [1024, 1024], P(('row', 'col')), may hold values 0 or 1
Outputs:
- pair_out: bfloat16 [1024, 1024, 128], P('row', 'col')
- loss: float32 [], replicated
- grad_gain: float32 [128], replicated
- grad_bias: float32 [128], replicated
- grad_gate: float32 [128, 512], replicated
- grad_up: float32 [128, 512], replicated
- grad_out: float32 [512, 128], replicated
- grad_head: float32 [128, 64], replicated
All inputs are finite; a program needn't handle non-finite values. No bound on the sum of `pair_mask` on one device may be relied on, other than what follows from the above.
Results may differ from a plain program's by a relative error of at most 0.001.
The roundings to bfloat16 on the way count: a program that leaves them out, or rounds other values in their place, can miss the bound.
Values may be sent and summed in bfloat16 or wider, within the bound.
No kernel may reach another device: no remote copies, remote signals or barrier semaphores. Data moves between devices by JAX's collectives and lax.ppermute only.
A program may use at most 64 MiB of HBM per device.

v0:
```python
import jax
import jax.numpy as jnp
from jax import lax
from jax.experimental import pallas as pl
from jax.experimental.pallas import tpu as pltpu
from jax.sharding import PartitionSpec as P


EPSILON = 1e-05
F32 = jnp.float32
BF16 = jnp.bfloat16
AXES = ("row", "col")

SIDE = 64
GROUP = 8
F_COLS = 32
B_GROUPS = 2
ROWS = SIDE * GROUP // 2
CHUNK_ROWS = SIDE * SIDE // 4

ROUTES = (((0, 1, 1), (0, 3, 3)), ((0, 2, 2), None))


def chip_of(device):
    r, c = divmod(device, 8)
    return (c // 2, (r % 8) // 2, (c % 2) * 2 + r // 8), r % 2


def device_at(chip, core):
    x, y, z = chip
    return ((z % 2) * 8 + y * 2 + core) * 8 + x * 2 + z // 2


def mirror_of(device, turn):
    r, c = divmod(device, 8)
    return (2 * c + (r + turn) % 2) * 8 + r // 2


def shifted(device, shift):
    chip, core = chip_of(device)
    return device_at(tuple((a + b) % 4 for a, b in zip(chip, shift)), core)


def send_to_mirror(value, turn, route):
    devices = range(128)
    if route is None:
        return lax.ppermute(value, AXES, [(d, mirror_of(d, turn)) for d in devices])
    value = lax.ppermute(value, AXES, [(d, shifted(d, route)) for d in devices])
    return lax.ppermute(value, AXES, [(shifted(d, route), mirror_of(d, turn)) for d in devices])


def dot(left, right, dims=((1,), (0,))):
    return lax.dot_general(left, right, (dims, ((), ())), preferred_element_type=F32)


NT = ((1,), (1,))
TN = ((0,), (0,))


def normalize(rows_in, gain, bias):
    values = rows_in.astype(F32)
    centered = values - jnp.mean(values, axis=-1, keepdims=True)
    variance = jnp.mean(centered * centered, axis=-1, keepdims=True)
    unit_rows = centered * lax.rsqrt(variance + EPSILON)
    return unit_rows, (unit_rows * gain + bias).astype(BF16)


def sigmoid(values):
    return 0.5 * jnp.tanh(0.5 * values) + 0.5


def head_square(head_t):
    blank = jnp.zeros_like(head_t)
    return jnp.concatenate(
        [
            jnp.concatenate([head_t, blank], axis=1),
            jnp.concatenate([blank, head_t], axis=1),
        ],
        axis=0,
    )


def block_words(words, block):
    tile = words[...]
    return jnp.where(block == 0, tile[:, :SIDE], tile[:, SIDE:])


def forward_body(chunks, core, pair, gain, bias, w_gate, w_up, w_out, head_t, *rest):
    pair_out, *sends = rest[-2 - len(chunks) : -1]
    wide = rest[-1]
    rows_in = pair[...].reshape(SIDE * F_COLS, 128)
    count = 4
    size = SIDE * F_COLS // count
    for k in range(count):
        part = rows_in[k * size : (k + 1) * size]
        _, normed = normalize(part, gain[...], bias[...])
        gate_pre = dot(normed, w_gate[...])
        up_pre = dot(normed, w_up[...])
        hidden = (gate_pre * sigmoid(gate_pre) * up_pre).astype(BF16)
        result = (part.astype(F32) + dot(hidden, w_out[...])).astype(BF16)
        pair_out[k * size // F_COLS : (k + 1) * size // F_COLS] = result.reshape(
            size // F_COLS, 1, F_COLS, 128
        )
        wide[k * size : (k + 1) * size, :] = result.astype(F32)
    head_two = head_square(head_t[...])
    halves = []
    for grp in range(F_COLS // GROUP):
        left, right = [
            jnp.concatenate(
                [
                    wide[pl.ds(grp * GROUP + shift + a, SIDE, stride=F_COLS), :]
                    for a in range(GROUP // 2)
                ],
                axis=0,
            )
            for shift in (0, GROUP // 2)
        ]
        both = jnp.concatenate([left, right], axis=1).astype(BF16)
        halves.append(dot(both, head_two, NT).astype(BF16))
    for k, chunk in enumerate(chunks):

        @pl.when(pl.program_id(0) == k)
        def _():
            sends[k][:CHUNK_ROWS, :] = jnp.concatenate(halves, axis=0)
            if chunk == 3:
                own = block_words(rest[0], lax.rem(core[0] + 1, 2))
                target = jnp.bitwise_and(own, 65535).astype(F32)
                mask = jnp.right_shift(own, 16).astype(F32)
                both = jnp.concatenate([target, mask], axis=1)
                sends[k][CHUNK_ROWS:, :] = both.astype(BF16)


def whole(a):
    return pl.BlockSpec(a.shape, lambda g, w: (0,) * len(a.shape))


def block_of(turn, core):
    return core[0] if turn == 0 else 1 - core[0]


def forward_call(core, chunks, pair4, weights, words=None, partial=None):
    block = pl.BlockSpec(
        (SIDE, 1, F_COLS, 128),
        lambda g, w: (
            0,
            lax.rem(w[0] + (g + chunks[0]) // 2, 2),
            lax.rem(g + chunks[0], 2),
            0,
        ),
    )
    in_specs = [block] + [whole(a) for a in weights]
    args = [pair4, *weights]
    alias = {}
    if words is not None:
        in_specs.append(whole(words))
        args.append(words)
    if partial is not None:
        in_specs.append(pl.BlockSpec(memory_space=pl.ANY))
        alias = {1 + len(args): 0}
        args.append(partial)
    sizes = [CHUNK_ROWS + (SIDE if chunk == 3 else 0) for chunk in chunks]
    outs = (jax.ShapeDtypeStruct(pair4.shape, BF16),) + tuple(
        jax.ShapeDtypeStruct((size, 128), BF16) for size in sizes
    )
    pairs = SIDE * F_COLS * len(chunks)

    def body(*refs):
        forward_body(chunks, *refs)

    return pl.pallas_call(
        body,
        out_shape=outs,
        grid_spec=pltpu.PrefetchScalarGridSpec(
            num_scalar_prefetch=1,
            grid=(len(chunks),),
            in_specs=in_specs,
            out_specs=(block,) + tuple(whole(a) for a in outs[1:]),
            scratch_shapes=[pltpu.VMEM((SIDE * F_COLS, 128), F32)],
        ),
        input_output_aliases=alias,
        cost_estimate=pl.CostEstimate(
            flops=pairs * 2 * 128 * 512 * 3, transcendentals=pairs * 512, bytes_accessed=pairs * 640
        ),
        compiler_params=pltpu.CompilerParams(
            dimension_semantics=("arbitrary",), vmem_limit_bytes=20 * 1024 * 1024
        ),
        name="forward",
    )(core, *args)


def backward_body(turn, first, last, core, *refs):
    pair, pair_out, mirror_a, mirror_b, mirror_words, words = refs[:6]
    gain, bias, w_gate, w_up, w_out, head_t = refs[6:12]
    rest = list(refs[12:])
    earlier = None
    if not first:
        earlier, rest = rest[:4], rest[4:]
    if last:
        keep, send = rest[:2]
        rest = rest[2:]
    g_in, g_out, g_head, g_small, s_normed, s_grad_in, s_hidden, s_pair = rest
    sums = (g_in, g_out, g_head, g_small)
    hid = w_out.shape[0]
    step = pl.program_id(0)

    @pl.when(step == 0)
    def _():
        for k, ref in enumerate(sums):
            ref[...] = jnp.zeros_like(ref) if first else earlier[k][...]

    lane = lax.broadcasted_iota(jnp.int32, (ROWS, 128), 1)
    wanted = (jnp.bitwise_and(lane, 63) + 64).astype(F32)
    lane_row = lax.broadcasted_iota(jnp.int32, (128, 128), 0)
    lane_col = lax.broadcasted_iota(jnp.int32, (128, 128), 1)
    same = (lane_row // 64 == lane_col // 64).astype(F32).astype(BF16)
    sum_bins = jnp.concatenate([same, same], axis=0)
    head_two = head_square(head_t[...])
    head_four = jnp.concatenate([head_two, head_two], axis=0)
    own = block_words(words, lax.rem(core[0] + turn, 2))
    own = jnp.bitwise_and(own, 65535) + 64 * jnp.right_shift(own, 16)
    own = own.astype(F32).astype(BF16)
    if turn == 0:
        other = block_words(mirror_words, core[0])
        other = jnp.bitwise_and(other, 65535) + 64 * jnp.right_shift(other, 16)
        other = other.astype(F32).astype(BF16)
    else:
        other = mirror_words[...].astype(F32)
        other = (other[:, :SIDE] + 64.0 * other[:, SIDE:]).astype(BF16)
    early = step < CHUNK_ROWS // (B_GROUPS * ROWS)
    pick_n = lax.broadcasted_iota(jnp.int32, (SIDE, 512), 1)
    pick_k = lax.broadcasted_iota(jnp.int32, (SIDE, 512), 0)
    pick_base = pick_n // 128 + (GROUP // 2) * (jnp.bitwise_and(pick_n, 127) // 64)

    for grp in range(B_GROUPS):
        at = slice(grp * 2 * ROWS, (grp + 1) * 2 * ROWS)
        x_out = pair_out[grp * GROUP : (grp + 1) * GROUP].reshape(2 * ROWS, 128)
        both = jnp.concatenate([x_out[:ROWS], x_out[ROWS:]], axis=1)
        half = dot(both, head_two, NT).astype(BF16)
        rows = slice(grp * ROWS, (grp + 1) * ROWS)
        mirror = jnp.where(early, mirror_a[rows, :].astype(F32), mirror_b[rows, :].astype(F32))
        logits = half.astype(F32) + mirror
        expo = 0.5 * jnp.exp(logits)
        high = expo.astype(BF16)
        low = (expo - high.astype(F32)).astype(BF16)
        total = dot(jnp.concatenate([high, low], axis=1), sum_bins)
        log_total = jnp.log(total) + 0.6931471805599453
        soft = jnp.exp(logits - log_total)
        group = step * B_GROUPS + grp
        pick = (pick_k == pick_base + GROUP * group).astype(F32).astype(BF16)
        codes = []
        for spread in (dot(own, pick, TN), dot(other, pick)):
            codes.append(
                jnp.concatenate([spread[:, 128 * a : 128 * (a + 1)] for a in range(4)], axis=0)
            )
        grads = [
            (
                (jnp.where(c >= 63.5, soft, 0.0) - jnp.where(c == wanted, 1.0, 0.0)) * (1.0 / 1024)
            ).astype(BF16)
            for c in codes
        ]
        loss_part = jnp.where(codes[0] == wanted, log_total - logits, 0.0)
        grad_both = jnp.concatenate(grads, axis=1)
        g_head[...] += dot(grad_both, both, TN)
        grad_pair = dot(grad_both, head_four).astype(BF16)
        grad_pair = jnp.concatenate([grad_pair[:, :128], grad_pair[:, 128:]], axis=0)
        s_pair[at, :] = grad_pair

        x_in = pair[grp * GROUP : (grp + 1) * GROUP].reshape(2 * ROWS, 128)
        unit_rows, normed = normalize(x_in, gain[...], bias[...])
        s_normed[at, :] = normed
        gate_pre = dot(normed, w_gate[...])
        up_pre = dot(normed, w_up[...])
        grad_hidden = dot(grad_pair, w_out[...], NT)
        squashed = sigmoid(gate_pre)
        silu_val = gate_pre * squashed
        s_hidden[at, :] = (silu_val * up_pre).astype(BF16)
        slope = squashed * (1.0 + gate_pre * (1.0 - squashed))
        s_grad_in[at, :hid] = (grad_hidden * up_pre * slope).astype(BF16)
        s_grad_in[at, hid:] = (grad_hidden * silu_val).astype(BF16)
        grad_normed = dot(s_grad_in[at, :hid], w_gate[...], NT)
        grad_normed += dot(s_grad_in[at, hid:], w_up[...], NT)
        fold = lambda v: jnp.sum(v.reshape(-1, 8, 128), axis=0)
        g_small[0:8, :] += fold(grad_normed * unit_rows)
        g_small[8:16, :] += fold(grad_normed)
        g_small[16:24, :] += fold(loss_part)
    g_in[...] += dot(s_normed[...], s_grad_in[...], TN)
    g_out[...] += dot(s_pair[...], s_hidden[...], TN)

    if not last:
        return

    def put_in(ref):
        for k in range(8):
            ref[128 * k : 128 * (k + 1), :] = g_in[:, 128 * k : 128 * (k + 1)]

    def put_rest(ref):
        for k in range(4):
            ref[128 * k : 128 * (k + 1), :] = g_out[:, 128 * k : 128 * (k + 1)].T
        ref[512:576, :] = (
            g_head[0:64, 0:128]
            + g_head[64:128, 128:256]
            + g_head[128:192, 0:128]
            + g_head[192:256, 128:256]
        )
        small = [jnp.sum(g_small[8 * k : 8 * k + 8, :], axis=0, keepdims=True) for k in range(3)]
        ref[576:584, :] = jnp.concatenate(small + [jnp.zeros((5, 128), F32)], axis=0)
        ref[584:1024, :] = jnp.zeros((440, 128), F32)

    at_end = step == pl.num_programs(0) - 1

    @pl.when(jnp.logical_and(at_end, core[0] == 0))
    def _():
        put_in(keep)
        put_rest(send)

    @pl.when(jnp.logical_and(at_end, core[0] != 0))
    def _():
        put_in(send)
        put_rest(keep)


def backward_call(
    core, turn, pair4, pair_out4, mirror_a, mirror_b, mirror_words, words, weights, earlier, last
):
    wide, hid = 2 * weights[2].shape[1], weights[4].shape[0]
    steps = SIDE // (GROUP * B_GROUPS)
    block = pl.BlockSpec(
        (GROUP * B_GROUPS, 1, SIDE, 128), lambda g, w: (g, block_of(turn, w), 0, 0)
    )
    rows = ROWS * B_GROUPS
    half_way = CHUNK_ROWS // rows
    fixed = (words, *weights)
    in_specs = [
        block,
        block,
        pl.BlockSpec((rows, 128), lambda g, w: (jnp.minimum(g, half_way - 1), 0)),
        pl.BlockSpec((rows, 128), lambda g, w: (jnp.maximum(g - half_way, 0), 0)),
        pl.BlockSpec((SIDE, 128), lambda g, w: (turn * CHUNK_ROWS // SIDE, 0)),
    ]
    in_specs += [whole(a) for a in fixed]
    args = [pair4, pair_out4, mirror_a, mirror_b, mirror_words, *fixed]
    sums = [(128, wide), (128, hid), (256, 256), (24, 128)]
    if earlier is not None:
        in_specs += [whole(a) for a in earlier]
        args += list(earlier)
    outs = [jax.ShapeDtypeStruct(s, F32) for s in ([(1024, 128)] * 2 if last else sums)]
    scratch = [pltpu.VMEM(s, F32) for s in sums] if last else []
    scratch += [
        pltpu.VMEM((2 * rows, 128), BF16),
        pltpu.VMEM((2 * rows, wide), BF16),
        pltpu.VMEM((2 * rows, hid), BF16),
        pltpu.VMEM((2 * rows, 128), BF16),
    ]
    pairs = SIDE * SIDE

    def body(*refs):
        backward_body(turn, earlier is None, last, *refs)

    return pl.pallas_call(
        body,
        out_shape=tuple(outs),
        grid_spec=pltpu.PrefetchScalarGridSpec(
            num_scalar_prefetch=1,
            grid=(steps,),
            in_specs=in_specs,
            out_specs=tuple(whole(a) for a in outs),
            scratch_shapes=scratch,
        ),
        cost_estimate=pl.CostEstimate(
            flops=pairs * 2 * 128 * 512 * 8, transcendentals=pairs * 640, bytes_accessed=pairs * 640
        ),
        compiler_params=pltpu.CompilerParams(
            dimension_semantics=("arbitrary",), vmem_limit_bytes=28 * 1024 * 1024
        ),
        name="backward",
    )(core, *args)


def unpack_body(core, mine, other, d_gate, d_up, d_out, d_head, d_gain, d_bias, loss):
    def fill(lower, upper):
        for k in range(4):
            d_gate[:, 128 * k : 128 * (k + 1)] = lower[128 * k : 128 * (k + 1), :]
            d_up[:, 128 * k : 128 * (k + 1)] = lower[512 + 128 * k : 640 + 128 * k, :]
        d_out[...] = upper[0:512, :]
        d_head[...] = upper[512:576, :]
        d_gain[...] = upper[576:577, :]
        d_bias[...] = upper[577:578, :]
        loss[0, 0] = jnp.sum(upper[578:579, :]) * (1.0 / 1048576)

    @pl.when(core[0] == 0)
    def _():
        fill(mine, other)

    @pl.when(core[0] != 0)
    def _():
        fill(other, mine)


def unpack_call(core, mine, other):
    shapes = [(128, 512), (128, 512), (512, 128), (64, 128), (1, 128), (1, 128), (1, 1)]
    outs = tuple(jax.ShapeDtypeStruct(s, F32) for s in shapes)
    specs = [whole(a) for a in outs[:-1]] + [pl.BlockSpec(memory_space=pltpu.SMEM)]
    return pl.pallas_call(
        unpack_body,
        out_shape=outs,
        grid_spec=pltpu.PrefetchScalarGridSpec(
            num_scalar_prefetch=1,
            grid=(1,),
            in_specs=[whole(mine), whole(other)],
            out_specs=tuple(specs),
        ),
        compiler_params=pltpu.CompilerParams(vmem_limit_bytes=8 * 1024 * 1024),
        name="unpack",
    )(core, mine, other)


def shards(
    pair, ln_gain, ln_bias, gate_weight, up_weight, out_weight, head_weight, targets, pair_mask
):
    rows_tile, _, width = pair.shape
    core = lax.rem(lax.axis_index("row"), 2).astype(jnp.int32).reshape(1)

    words = targets + 65536 * pair_mask
    tile_words = lax.all_to_all(words, "col", split_axis=1, concat_axis=0, tiled=True)

    pair4 = pair.reshape(rows_tile, 2, SIDE, width)
    weights = (
        ln_gain.reshape(1, width),
        ln_bias.reshape(1, width),
        gate_weight,
        up_weight,
        out_weight,
        head_weight.T,
    )
    in_hbm = lambda a: pltpu.with_memory_space_constraint(a, pltpu.HBM)
    out4, *sent = forward_call(core, (0, 1, 2), in_hbm(pair4), [in_hbm(a) for a in weights])
    words0 = send_to_mirror(tile_words, 0, None)
    out4, last = forward_call(core, (3,), pair4, weights, tile_words, out4)
    mirror = [send_to_mirror(v, k // 2, ROUTES[k // 2][k % 2]) for k, v in enumerate((*sent, last))]
    mirror0, mirror1 = mirror[:2], mirror[2:]
    held = in_hbm(out4)
    sums = backward_call(core, 0, pair4, held, *mirror0, words0, tile_words, weights, None, False)
    keep, send = backward_call(
        core, 1, pair4, held, *mirror1, mirror1[1], tile_words, weights, sums, True
    )
    sibling = [(d, device_at(chip_of(d)[0], 1 - chip_of(d)[1])) for d in range(128)]
    groups = [[d for d in range(128) if chip_of(d)[1] == k] for k in range(2)]
    both_cores = (keep + lax.ppermute(send, AXES, sibling)).reshape(64, 16, 128)
    pieces = lax.all_to_all(
        both_cores, AXES, split_axis=0, concat_axis=0, axis_index_groups=groups, tiled=True
    )
    mine = jnp.sum(pieces, axis=0, keepdims=True)
    mine = lax.all_to_all(
        jnp.broadcast_to(mine, pieces.shape),
        AXES,
        split_axis=0,
        concat_axis=0,
        axis_index_groups=groups,
        tiled=True,
    ).reshape(1024, 128)
    other = lax.ppermute(mine, AXES, sibling)
    d_gate, d_up, d_out, d_head, d_gain, d_bias, loss = unpack_call(core, mine, other)
    return (
        out4.reshape(pair.shape),
        loss.reshape(()),
        d_gain.reshape(width),
        d_bias.reshape(width),
        d_gate,
        d_up,
        d_out,
        d_head.T,
    )


def solution(mesh):
    placed = (
        P("row", "col", None),
        P(),
        P(),
        P(),
        P(),
        P(),
        P(),
        P(AXES, None),
        P(AXES, None),
    )
    return jax.shard_map(
        shards,
        mesh=mesh,
        in_specs=placed,
        out_specs=(P("row", "col", None), P(), P(), P(), P(), P(), P(), P()),
        check_vma=False,
    )
```

profile of v0, /device:TPU:1, one launch (start us, length us, event | category | flops | bytes accessed | tf_op | source)
XLA Modules:
  0.0 146.4 jit_solution(17700663043609347716)
XLA Ops:
  0.6 0.0 copy-start.7
  0.7 0.0 copy-start.8
  0.7 11.0 %forward.2 = (bf16[64,2,64,128]{3,2,1,0:T(8,128)(2,1)}, bf16[1024,128]{1,0:T(8,128)(2,1)S(1)}, bf16[1024,128]{1,0:T(8,128)(2,1)S(1)}, bf16[1024,128]{1,0:T(8,128)(2,1)S(1)}) custom-call(s32[1]{0:T(128)} %bitcast.refs_0_.core, bf16[64,2,64,128]{3,2,1,0:T(8,128)(2,1)} %bitcast.19, f32[1,128]{1,0:T(1,128)} %bitcast.31, f32[1,128]{1,0:T(1,128)} %bitcast.35, ...), custom_call_target="tpu_custom_call" | custom-call | flops 2415919104 | bytes 3932160 | tf_op jit(solution)/shard_map/forward/pallas_call | solution.py:170
  11.7 3.5 %collective-permute-start.3 = (bf16[1024,128]{1,0:T(8,128)(2,1)S(1)}, bf16[1024,128]{1,0:T(8,128)(2,1)S(1)}, u32[]{:S(2)}, u32[]{:S(2)}) collective-permute-start(bf16[1024,128]{1,0:T(8,128)(2,1)S(1)} %get-tuple-element.31), channel_id=1, source_target_pairs={{0,80},{1,81},{2,82},{3,83},{4,84},{5,85},{6,86},{7,87},{8,88},{9,... | collective-permute-start | bytes 786440 | tf_op jit(solution)/shard_map/ppermute | solution.py:48
  15.2 3.6 %collective-permute-start.5 = (bf16[1024,128]{1,0:T(8,128)(2,1)S(1)}, bf16[1024,128]{1,0:T(8,128)(2,1)S(1)}, u32[]{:S(2)}, u32[]{:S(2)}) collective-permute-start(bf16[1024,128]{1,0:T(8,128)(2,1)S(1)} %get-tuple-element.32), channel_id=1, source_target_pairs={{0,113},{1,112},{2,115},{3,114},{4,117},{5,116},{6,119},{7,118},{8... | collective-permute-start | bytes 786440 | tf_op jit(solution)/shard_map/ppermute | solution.py:48
  18.7 2.4 %collective-permute-start = (bf16[1024,128]{1,0:T(8,128)(2,1)S(1)}, bf16[1024,128]{1,0:T(8,128)(2,1)S(1)}, u32[]{:S(2)}, u32[]{:S(2)}) collective-permute-start(bf16[1024,128]{1,0:T(8,128)(2,1)S(1)} %get-tuple-element.29), channel_id=1, source_target_pairs={{0,33},{1,32},{2,35},{3,34},{4,37},{5,36},{6,39},{7,38},{8,41},{9,... | collective-permute-start | bytes 786440 | tf_op jit(solution)/shard_map/ppermute | solution.py:48
  21.1 3.6 %collective-permute-done.3 = bf16[1024,128]{1,0:T(8,128)(2,1)S(1)} collective-permute-done((bf16[1024,128]{1,0:T(8,128)(2,1)S(1)}, bf16[1024,128]{1,0:T(8,128)(2,1)S(1)}, u32[]{:S(2)}, u32[]{:S(2)}) %collective-permute-start.3) | collective-permute-done | bytes 262176 | tf_op jit(solution)/shard_map/ppermute | solution.py:48
  24.8 2.7 %collective-permute-start.4 = (bf16[1024,128]{1,0:T(8,128)(2,1)S(1)}, bf16[1024,128]{1,0:T(8,128)(2,1)S(1)}, u32[]{:S(2)}, u32[]{:S(2)}) collective-permute-start(bf16[1024,128]{1,0:T(8,128)(2,1)S(1)} %collective-permute-done.3), channel_id=1, source_target_pairs={{80,0},{81,16},{82,32},{83,48},{84,64},{85,80},{86,96},{87,112},{8... | collective-permute-start | bytes 786440 | tf_op jit(solution)/shard_map/ppermute | solution.py:49
  27.4 0.0 collective-permute-done.5
  27.4 2.4 %collective-permute-start.6 = (bf16[1024,128]{1,0:T(8,128)(2,1)S(1)}, bf16[1024,128]{1,0:T(8,128)(2,1)S(1)}, u32[]{:S(2)}, u32[]{:S(2)}) collective-permute-start(bf16[1024,128]{1,0:T(8,128)(2,1)S(1)} %collective-permute-done.5), channel_id=1, source_target_pairs={{113,0},{112,16},{115,32},{114,48},{117,64},{116,80},{119,96},{118... | collective-permute-start | bytes 786440 | tf_op jit(solution)/shard_map/ppermute | solution.py:49
  29.9 18.4 %all_to_all.29 = s32[8,8,128]{2,0,1:T(8,128)S(1)} all-to-all(s32[8,8,128]{2,0,1:T(8,128)S(1)} %add_bitcast_fusion), channel_id=1, replica_groups=mesh['row'=16,'col'=8] {'col'}, dimensions={1} | all-to-all | bytes 65536 | tf_op jit(solution)/shard_map/all_to_all | solution.py:424
  48.3 0.7 collective-permute-start.7
  49.0 3.8 %forward.3 = (bf16[64,2,64,128]{3,2,1,0:T(8,128)(2,1)}, bf16[1088,128]{1,0:T(8,128)(2,1)S(1)}) custom-call(s32[1]{0:T(128)} %bitcast.refs_0_.core, bf16[64,2,64,128]{3,2,1,0:T(8,128)(2,1)S(1)} %bitcast.20, f32[1,128]{1,0:T(1,128)S(1)} %bitcast.32, f32[1,128]{1,0:T(1,128)S(1)} %bitcast.36, ...), custom_call_target="tpu_custom_call", output_to_operand_aliasing={{0}: (9, {})} | custom-call | flops 805306368 | bytes 1310720 | tf_op jit(solution)/shard_map/forward/pallas_call | solution.py:170
  52.8 12.4 %collective-permute-start.2 = (bf16[1088,128]{1,0:T(8,128)(2,1)S(1)}, bf16[1088,128]{1,0:T(8,128)(2,1)S(1)}, u32[]{:S(2)}, u32[]{:S(2)}) collective-permute-start(bf16[1088,128]{1,0:T(8,128)(2,1)S(1)} %get-tuple-element.30), channel_id=1, source_target_pairs={{0,8},{1,24},{2,40},{3,56},{4,72},{5,88},{6,104},{7,120},{8,0},{9,... | collective-permute-start | bytes 835592 | tf_op jit(solution)/shard_map/ppermute | solution.py:47
  65.2 0.0 collective-permute-done
  65.2 0.0 collective-permute-start.1
  65.2 0.0 collective-permute-done.7.refs_5_
  65.2 0.0 collective-permute-done.4.refs_3_
  65.2 0.0 collective-permute-done.6.refs_4_
  65.2 13.8 %backward.2 = (f32[128,1024]{1,0:T(8,128)S(1)}, f32[128,512]{1,0:T(8,128)S(1)}, f32[256,256]{1,0:T(8,128)S(1)}, f32[24,128]{1,0:T(8,128)S(1)}) custom-call(s32[1]{0:T(128)} %bitcast.refs_0_.core, bf16[64,2,64,128]{3,2,1,0:T(8,128)(2,1)S(1)} %bitcast.21, bf16[64,2,64,128]{3,2,1,0:T(8,128)(2,1)} %get-tuple-element.28.refs_2_, ...), custom_call_target="tpu_custom_call" | custom-call | flops 4294967296 | bytes 2621440 | tf_op jit(solution)/shard_map/backward/pallas_call | solution.py:359
  79.1 0.0 collective-permute-done.2.refs_4_.refs_5_
  79.1 9.3 %collective-permute-done.1.refs_3_ = bf16[1024,128]{1,0:T(8,128)(2,1)S(1)} collective-permute-done((bf16[1024,128]{1,0:T(8,128)(2,1)S(1)}, bf16[1024,128]{1,0:T(8,128)(2,1)S(1)}, u32[]{:S(2)}, u32[]{:S(2)}) %collective-permute-start.1) | collective-permute-done | bytes 262176 | tf_op jit(solution)/shard_map/ppermute | solution.py:49
  88.3 14.0 %backward.3 = (f32[1024,128]{1,0:T(8,128)S(1)}, f32[1024,128]{1,0:T(8,128)S(1)}) custom-call(s32[1]{0:T(128)} %bitcast.refs_0_.core, bf16[64,2,64,128]{3,2,1,0:T(8,128)(2,1)S(1)} %bitcast.22, bf16[64,2,64,128]{3,2,1,0:T(8,128)(2,1)} %get-tuple-element.28.refs_2_, bf16[1024,128]{1,0:T(8,128)(2,1)S(1)} %collective-permute-done.1.refs_3_, ...), custom_call_target="tpu_custom_call" | custom-call | flops 4294967296 | bytes 2621440 | tf_op jit(solution)/shard_map/backward/pallas_call | solution.py:359
  102.3 0.1 collective-permute-start.8
  102.4 1.9 %collective-permute-done.8 = f32[1024,128]{1,0:T(8,128)S(1)} collective-permute-done((f32[1024,128]{1,0:T(8,128)S(1)}, f32[1024,128]{1,0:T(8,128)S(1)}, u32[]{:S(2)}, u32[]{:S(2)}) %collective-permute-start.8) | collective-permute-done | bytes 524320 | tf_op jit(solution)/shard_map/ppermute | solution.py:448
  104.3 0.1 add.7
  104.4 20.4 %all_to_all.30 = f32[64,16,128]{2,1,0:T(8,128)S(1)} all-to-all(f32[64,16,128]{2,1,0:T(8,128)S(1)} %bitcast.39), channel_id=1, replica_groups={{0,1,2,3,4,5,6,7,16,17,18,19,20,21,22,23,32,33,34,35,36,37,38,39,48,49,..., dimensions={0} | all-to-all | bytes 1048576 | tf_op jit(solution)/shard_map/all_to_all | solution.py:449
  124.7 0.1 reduce_sum.9
  124.8 15.3 %all_to_all.31 = f32[64,16,128]{2,1,0:T(8,128)S(1)} all-to-all(f32[64,16,128]{2,1,0:T(8,128)S(1)} %broadcast_in_dim.2), channel_id=1, replica_groups={{0,1,2,3,4,5,6,7,16,17,18,19,20,21,22,23,32,33,34,35,36,37,38,39,48,49,..., dimensions={0} | all-to-all | bytes 1048576 | tf_op jit(solution)/shard_map/all_to_all | solution.py:453
  140.2 3.4 %collective-permute-start.9 = (f32[1024,128]{1,0:T(8,128)S(1)}, f32[1024,128]{1,0:T(8,128)S(1)}, u32[]{:S(2)}, u32[]{:S(2)}) collective-permute-start(f32[1024,128]{1,0:T(8,128)S(1)} %bitcast.17), channel_id=1, source_target_pairs={{0,8},{1,9},{2,10},{3,11},{4,12},{5,13},{6,14},{7,15},{8,0},{9,1},... | collective-permute-start | bytes 1572872 | tf_op jit(solution)/shard_map/ppermute | solution.py:461
  143.6 1.5 %collective-permute-done.9.other = f32[1024,128]{1,0:T(8,128)S(1)} collective-permute-done((f32[1024,128]{1,0:T(8,128)S(1)}, f32[1024,128]{1,0:T(8,128)S(1)}, u32[]{:S(2)}, u32[]{:S(2)}) %collective-permute-start.9) | collective-permute-done | bytes 524320 | tf_op jit(solution)/shard_map/ppermute | solution.py:461
  145.1 1.1 unpack.1
  (18 shorter events, 0.1 us)
Async XLA Ops:
  0.6 29.2 %copy-start.7 = (s32[8,1024]{1,0:T(8,128)S(1)}, s32[8,1024]{1,0:T(8,128)}, u32[]{:S(2)}) copy-start(s32[8,1024]{1,0:T(8,128)} %param.16) | copy-start | bytes 98308
  0.7 29.2 %copy-start.8 = (s32[8,1024]{1,0:T(8,128)S(1)}, s32[8,1024]{1,0:T(8,128)}, u32[]{:S(2)}) copy-start(s32[8,1024]{1,0:T(8,128)} %param.17) | copy-start | bytes 98308
  0.7 48.3 %copy-start = (bf16[64,128,128]{2,1,0:T(8,128)(2,1)S(1)}, bf16[64,128,128]{2,1,0:T(8,128)(2,1)}, u32[]{:S(2)}) copy-start(bf16[64,128,128]{2,1,0:T(8,128)(2,1)} %param.9) | copy-start | bytes 6291460
  0.7 48.3 %copy-start.1 = (bf16[128,512]{1,0:T(8,128)(2,1)S(1)}, bf16[128,512]{1,0:T(8,128)(2,1)}, u32[]{:S(2)}) copy-start(bf16[128,512]{1,0:T(8,128)(2,1)} %refs_9_.3) | copy-start | bytes 393220
  0.7 48.3 %copy-start.2 = (bf16[128,512]{1,0:T(8,128)(2,1)S(1)}, bf16[128,512]{1,0:T(8,128)(2,1)}, u32[]{:S(2)}) copy-start(bf16[128,512]{1,0:T(8,128)(2,1)} %refs_10_.3) | copy-start | bytes 393220
  0.7 48.3 %copy-start.3 = (bf16[512,128]{1,0:T(8,128)(2,1)S(1)}, bf16[512,128]{1,0:T(8,128)(2,1)}, u32[]{:S(2)}) copy-start(bf16[512,128]{1,0:T(8,128)(2,1)} %refs_11_.3) | copy-start | bytes 393220
  0.7 48.3 %copy-start.4 = (bf16[128,64]{0,1:T(8,128)(2,1)S(1)}, bf16[128,64]{0,1:T(8,128)(2,1)}, u32[]{:S(2)}) copy-start(bf16[128,64]{0,1:T(8,128)(2,1)} %param.15) | copy-start | bytes 49156
  0.7 48.3 %copy-start.5 = (f32[128]{0:T(128)S(1)}, f32[128]{0:T(128)}, u32[]{:S(2)}) copy-start(f32[128]{0:T(128)} %param.10) | copy-start | bytes 1540
  0.7 48.3 %copy-start.6 = (f32[128]{0:T(128)S(1)}, f32[128]{0:T(128)}, u32[]{:S(2)}) copy-start(f32[128]{0:T(128)} %param.11) | copy-start | bytes 1540
  11.7 13.0 %collective-permute-start.3 = (bf16[1024,128]{1,0:T(8,128)(2,1)S(1)}, bf16[1024,128]{1,0:T(8,128)(2,1)S(1)}, u32[]{:S(2)}, u32[]{:S(2)}) collective-permute-start(bf16[1024,128]{1,0:T(8,128)(2,1)S(1)} %get-tuple-element.31), channel_id=1, source_target_pairs={{0,80},{1,81},{2,82},{3,83},{4,84},{5,85},{6,86},{7,87},{8,88},{9,... | collective-permute-start | bytes 786440 | tf_op jit(solution)/shard_map/ppermute | solution.py:48
  15.2 12.2 %collective-permute-start.5 = (bf16[1024,128]{1,0:T(8,128)(2,1)S(1)}, bf16[1024,128]{1,0:T(8,128)(2,1)S(1)}, u32[]{:S(2)}, u32[]{:S(2)}) collective-permute-start(bf16[1024,128]{1,0:T(8,128)(2,1)S(1)} %get-tuple-element.32), channel_id=1, source_target_pairs={{0,113},{1,112},{2,115},{3,114},{4,117},{5,116},{6,119},{7,118},{8... | collective-permute-start | bytes 786440 | tf_op jit(solution)/shard_map/ppermute | solution.py:48
  18.7 46.4 %collective-permute-start = (bf16[1024,128]{1,0:T(8,128)(2,1)S(1)}, bf16[1024,128]{1,0:T(8,128)(2,1)S(1)}, u32[]{:S(2)}, u32[]{:S(2)}) collective-permute-start(bf16[1024,128]{1,0:T(8,128)(2,1)S(1)} %get-tuple-element.29), channel_id=1, source_target_pairs={{0,33},{1,32},{2,35},{3,34},{4,37},{5,36},{6,39},{7,38},{8,41},{9,... | collective-permute-start | bytes 786440 | tf_op jit(solution)/shard_map/ppermute | solution.py:48
  24.8 40.4 %collective-permute-start.4 = (bf16[1024,128]{1,0:T(8,128)(2,1)S(1)}, bf16[1024,128]{1,0:T(8,128)(2,1)S(1)}, u32[]{:S(2)}, u32[]{:S(2)}) collective-permute-start(bf16[1024,128]{1,0:T(8,128)(2,1)S(1)} %collective-permute-done.3), channel_id=1, source_target_pairs={{80,0},{81,16},{82,32},{83,48},{84,64},{85,80},{86,96},{87,112},{8... | collective-permute-start | bytes 786440 | tf_op jit(solution)/shard_map/ppermute | solution.py:49
  27.4 37.8 %collective-permute-start.6 = (bf16[1024,128]{1,0:T(8,128)(2,1)S(1)}, bf16[1024,128]{1,0:T(8,128)(2,1)S(1)}, u32[]{:S(2)}, u32[]{:S(2)}) collective-permute-start(bf16[1024,128]{1,0:T(8,128)(2,1)S(1)} %collective-permute-done.5), channel_id=1, source_target_pairs={{113,0},{112,16},{115,32},{114,48},{117,64},{116,80},{119,96},{118... | collective-permute-start | bytes 786440 | tf_op jit(solution)/shard_map/ppermute | solution.py:49
  48.3 16.9 %collective-permute-start.7 = (s32[64,128]{1,0:T(8,128)S(1)}, s32[64,128]{1,0:T(8,128)S(1)}, u32[]{:S(2)}, u32[]{:S(2)}) collective-permute-start(s32[64,128]{1,0:T(8,128)S(1)} %bitcast.23), channel_id=1, source_target_pairs={{0,0},{1,16},{2,32},{3,48},{4,64},{5,80},{6,96},{7,112},{8,8},{9,2... | collective-permute-start | bytes 98312 | tf_op jit(solution)/shard_map/ppermute | solution.py:47
  52.8 26.3 %collective-permute-start.2 = (bf16[1088,128]{1,0:T(8,128)(2,1)S(1)}, bf16[1088,128]{1,0:T(8,128)(2,1)S(1)}, u32[]{:S(2)}, u32[]{:S(2)}) collective-permute-start(bf16[1088,128]{1,0:T(8,128)(2,1)S(1)} %get-tuple-element.30), channel_id=1, source_target_pairs={{0,8},{1,24},{2,40},{3,56},{4,72},{5,88},{6,104},{7,120},{8,0},{9,... | collective-permute-start | bytes 835592 | tf_op jit(solution)/shard_map/ppermute | solution.py:47
  65.2 23.2 %collective-permute-start.1 = (bf16[1024,128]{1,0:T(8,128)(2,1)S(1)}, bf16[1024,128]{1,0:T(8,128)(2,1)S(1)}, u32[]{:S(2)}, u32[]{:S(2)}) collective-permute-start(bf16[1024,128]{1,0:T(8,128)(2,1)S(1)} %collective-permute-done), channel_id=1, source_target_pairs={{33,8},{32,24},{35,40},{34,56},{37,72},{36,88},{39,104},{38,120},{... | collective-permute-start | bytes 786440 | tf_op jit(solution)/shard_map/ppermute | solution.py:49
  102.3 2.0 %collective-permute-start.8 = (f32[1024,128]{1,0:T(8,128)S(1)}, f32[1024,128]{1,0:T(8,128)S(1)}, u32[]{:S(2)}, u32[]{:S(2)}) collective-permute-start(f32[1024,128]{1,0:T(8,128)S(1)} %get-tuple-element.38), channel_id=1, source_target_pairs={{0,8},{1,9},{2,10},{3,11},{4,12},{5,13},{6,14},{7,15},{8,0},{9,1},... | collective-permute-start | bytes 1572872 | tf_op jit(solution)/shard_map/ppermute | solution.py:448
  140.2 4.9 %collective-permute-start.9 = (f32[1024,128]{1,0:T(8,128)S(1)}, f32[1024,128]{1,0:T(8,128)S(1)}, u32[]{:S(2)}, u32[]{:S(2)}) collective-permute-start(f32[1024,128]{1,0:T(8,128)S(1)} %bitcast.17), channel_id=1, source_target_pairs={{0,8},{1,9},{2,10},{3,11},{4,12},{5,13},{6,14},{7,15},{8,0},{9,1},... | collective-permute-start | bytes 1572872 | tf_op jit(solution)/shard_map/ppermute | solution.py:461
where the time goes:
time: 147 us; the launch traced here: 146 us
  blocking collectives  54.1 us (37%)
  Pallas kernels  43.7 us (30%)
  starting transfers between devices  31 us (21%)
  waiting for transfers between devices  16.3 us (11%)
    pallas_call x2, Pallas kernels, backward_call(): pl.pallas_call(body, out_shape=tuple(outs), grid_spec=pltpu.PrefetchScala...  27.8 us
    all_to_all x1, blocking collectives, shards(): lax.all_to_all(both_cores, AXES, split_axis=0, concat_axis=0, axis_index_...  20.4 us
    all_to_all x1, blocking collectives, shards(): lax.all_to_all(words, 'col', split_axis=1, concat_axis=0, tiled=True)  18.4 us
    all_to_all x1, blocking collectives, shards(): lax.all_to_all(jnp.broadcast_to(mine, pieces.shape), AXES, split_axis=0,...  15.3 us
    pallas_call x2, Pallas kernels, forward_call(): pl.pallas_call(body, out_shape=outs, grid_spec=pltpu.PrefetchScalarGridSp...  14.8 us
    ppermute x2, starting transfers between devices, send_to_mirror(): return lax.ppermute(value, AXES, [(d, mirror_of(d, turn)) for d in devices])  13 us
    ppermute x3, starting transfers between devices, send_to_mirror(): value = lax.ppermute(value, AXES, [(d, shifted(d, route)) for d in devices])  9.41 us
    ppermute x3, waiting for transfers between devices, send_to_mirror(): lax.ppermute(value, AXES, [(shifted(d, route), mirror_of(d, turn)) for d...  9.27 us
  transfers between devices with their start and end apart: 10, of which 4 were waited for; matrix products, arithmetic and copies ran while one was open for 0% of the time, Pallas kernels for 12%

commit v1 on v0

--- a/solution.py
+++ b/solution.py
@@ -117,17 +117,11 @@
         ]
         both = jnp.concatenate([left, right], axis=1).astype(BF16)
         halves.append(dot(both, head_two, NT).astype(BF16))
-    for k, chunk in enumerate(chunks):
+    for k in range(len(chunks)):
 
         @pl.when(pl.program_id(0) == k)
         def _():
-            sends[k][:CHUNK_ROWS, :] = jnp.concatenate(halves, axis=0)
-            if chunk == 3:
-                own = block_words(rest[0], lax.rem(core[0] + 1, 2))
-                target = jnp.bitwise_and(own, 65535).astype(F32)
-                mask = jnp.right_shift(own, 16).astype(F32)
-                both = jnp.concatenate([target, mask], axis=1)
-                sends[k][CHUNK_ROWS:, :] = both.astype(BF16)
+            sends[k][...] = jnp.concatenate(halves, axis=0)
 
 
 def whole(a):
@@ -138,7 +132,7 @@
     return core[0] if turn == 0 else 1 - core[0]
 
 
-def forward_call(core, chunks, pair4, weights, words=None, partial=None):
+def forward_call(core, chunks, pair4, weights):
     block = pl.BlockSpec(
         (SIDE, 1, F_COLS, 128),
         lambda g, w: (
@@ -150,17 +144,8 @@
     )
     in_specs = [block] + [whole(a) for a in weights]
     args = [pair4, *weights]
-    alias = {}
-    if words is not None:
-        in_specs.append(whole(words))
-        args.append(words)
-    if partial is not None:
-        in_specs.append(pl.BlockSpec(memory_space=pl.ANY))
-        alias = {1 + len(args): 0}
-        args.append(partial)
-    sizes = [CHUNK_ROWS + (SIDE if chunk == 3 else 0) for chunk in chunks]
     outs = (jax.ShapeDtypeStruct(pair4.shape, BF16),) + tuple(
-        jax.ShapeDtypeStruct((size, 128), BF16) for size in sizes
+        jax.ShapeDtypeStruct((CHUNK_ROWS, 128), BF16) for _ in chunks
     )
     pairs = SIDE * F_COLS * len(chunks)
 
@@ -177,12 +162,11 @@
             out_specs=(block,) + tuple(whole(a) for a in outs[1:]),
             scratch_shapes=[pltpu.VMEM((SIDE * F_COLS, 128), F32)],
         ),
-        input_output_aliases=alias,
         cost_estimate=pl.CostEstimate(
             flops=pairs * 2 * 128 * 512 * 3, transcendentals=pairs * 512, bytes_accessed=pairs * 640
         ),
         compiler_params=pltpu.CompilerParams(
-            dimension_semantics=("arbitrary",), vmem_limit_bytes=20 * 1024 * 1024
+            dimension_semantics=("arbitrary",), vmem_limit_bytes=24 * 1024 * 1024
         ),
         name="forward",
     )(core, *args)
@@ -219,13 +203,9 @@
     own = block_words(words, lax.rem(core[0] + turn, 2))
     own = jnp.bitwise_and(own, 65535) + 64 * jnp.right_shift(own, 16)
     own = own.astype(F32).astype(BF16)
-    if turn == 0:
-        other = block_words(mirror_words, core[0])
-        other = jnp.bitwise_and(other, 65535) + 64 * jnp.right_shift(other, 16)
-        other = other.astype(F32).astype(BF16)
-    else:
-        other = mirror_words[...].astype(F32)
-        other = (other[:, :SIDE] + 64.0 * other[:, SIDE:]).astype(BF16)
+    other = block_words(mirror_words, core[0])
+    other = jnp.bitwise_and(other, 65535) + 64 * jnp.right_shift(other, 16)
+    other = other.astype(F32).astype(BF16)
     early = step < CHUNK_ROWS // (B_GROUPS * ROWS)
     pick_n = lax.broadcasted_iota(jnp.int32, (SIDE, 512), 1)
     pick_k = lax.broadcasted_iota(jnp.int32, (SIDE, 512), 0)
@@ -335,7 +315,7 @@
         block,
         pl.BlockSpec((rows, 128), lambda g, w: (jnp.minimum(g, half_way - 1), 0)),
         pl.BlockSpec((rows, 128), lambda g, w: (jnp.maximum(g - half_way, 0), 0)),
-        pl.BlockSpec((SIDE, 128), lambda g, w: (turn * CHUNK_ROWS // SIDE, 0)),
+        pl.BlockSpec((SIDE, 128), lambda g, w: (0, 0)),
     ]
     in_specs += [whole(a) for a in fixed]
     args = [pair4, pair_out4, mirror_a, mirror_b, mirror_words, *fixed]
@@ -433,15 +413,16 @@
         head_weight.T,
     )
     in_hbm = lambda a: pltpu.with_memory_space_constraint(a, pltpu.HBM)
-    out4, *sent = forward_call(core, (0, 1, 2), in_hbm(pair4), [in_hbm(a) for a in weights])
-    words0 = send_to_mirror(tile_words, 0, None)
-    out4, last = forward_call(core, (3,), pair4, weights, tile_words, out4)
-    mirror = [send_to_mirror(v, k // 2, ROUTES[k // 2][k % 2]) for k, v in enumerate((*sent, last))]
+    out4, *sent = forward_call(
+        core, (0, 1, 2, 3), in_hbm(pair4), [in_hbm(a) for a in weights]
+    )
+    mirror = [send_to_mirror(v, k // 2, ROUTES[k // 2][k % 2]) for k, v in enumerate(sent)]
     mirror0, mirror1 = mirror[:2], mirror[2:]
+    words0, words1 = [send_to_mirror(tile_words, k, None) for k in range(2)]
     held = in_hbm(out4)
     sums = backward_call(core, 0, pair4, held, *mirror0, words0, tile_words, weights, None, False)
     keep, send = backward_call(
-        core, 1, pair4, held, *mirror1, mirror1[1], tile_words, weights, sums, True
+        core, 1, pair4, held, *mirror1, words1, tile_words, weights, sums, True
     )
     sibling = [(d, device_at(chip_of(d)[0], 1 - chip_of(d)[1])) for d in range(128)]
     groups = [[d for d in range(128) if chip_of(d)[1] == k] for k in range(2)]

time: 147 us -> 153 us (1.041)
  blocking collectives: 54.1 us -> 64.2 us
  waiting for transfers between devices: 16.3 us -> 7.08 us
  starting transfers between devices: 31 us -> 37.2 us
    all_to_all x1, blocking collectives: 20.4 us -> 30.5 us  [shards(): lax.all_to_all(both_cores, AXES, split_axis=0, concat_axis=0, axis_index_...]
    ppermute x3, waiting for transfers between devices: 9.27 us -> 0.01 us  [send_to_mirror(): lax.ppermute(value, AXES, [(shifted(d, route), mirror_of(d, turn)) for d...]
    ppermute x3, starting transfers between devices: 5.12 us -> 11.1 us  [send_to_mirror(): lax.ppermute(value, AXES, [(shifted(d, route), mirror_of(d, turn)) for d...]
    pallas_call x2 -> x1, Pallas kernels: 14.8 us -> 14 us  [forward_call(): pl.pallas_call(body, out_shape=outs, grid_spec=pltpu.PrefetchScalarGridSp...]
    ppermute x2 -> x3, starting transfers between devices: 13 us -> 13.2 us  [send_to_mirror(): return lax.ppermute(value, AXES, [(d, mirror_of(d, turn)) for d in devices])]
  transfers between devices with their start and end apart: 10 -> 11, of which waited for: 4 -> 3; matrix products, arithmetic and copies ran while one was open for 0% -> 0% of each run, Pallas kernels for 12% -> 9%
where the time goes in v1:
time: 153 us
  blocking collectives  64.2 us (42%)
  Pallas kernels  42.9 us (28%)
  starting transfers between devices  37.2 us (24%)
  waiting for transfers between devices  7.08 us (5%)
    all_to_all x1, blocking collectives, shards(): lax.all_to_all(both_cores, AXES, split_axis=0, concat_axis=0, axis_index_...  30.5 us
    pallas_call x2, Pallas kernels, backward_call(): pl.pallas_call(body, out_shape=tuple(outs), grid_spec=pltpu.PrefetchScala...  27.9 us
    all_to_all x1, blocking collectives, shards(): lax.all_to_all(words, 'col', split_axis=1, concat_axis=0, tiled=True)  18.4 us
    all_to_all x1, blocking collectives, shards(): lax.all_to_all(jnp.broadcast_to(mine, pieces.shape), AXES, split_axis=0,...  15.3 us
    pallas_call x1, Pallas kernels, forward_call(): pl.pallas_call(body, out_shape=outs, grid_spec=pltpu.PrefetchScalarGridSp...  14 us
    ppermute x3, starting transfers between devices, send_to_mirror(): return lax.ppermute(value, AXES, [(d, mirror_of(d, turn)) for d in devices])  13.2 us
    ppermute x3, starting transfers between devices, send_to_mirror(): lax.ppermute(value, AXES, [(shifted(d, route), mirror_of(d, turn)) for d...  11.1 us
    ppermute x3, starting transfers between devices, send_to_mirror(): value = lax.ppermute(value, AXES, [(d, shifted(d, route)) for d in devices])  9.4 us
  transfers between devices with their start and end apart: 11, of which 3 were waited for; matrix products, arithmetic and copies ran while one was open for 0% of the time, Pallas kernels for 9%

profile of v1, /device:TPU:1, one launch (start us, length us, event | category | flops | bytes accessed | tf_op | source)
XLA Modules:
  0.0 152.7 jit_solution(471025612320773254)
XLA Ops:
  0.6 0.0 copy-start.7
  0.7 14.0 %forward.1 = (bf16[64,2,64,128]{3,2,1,0:T(8,128)(2,1)}, bf16[1024,128]{1,0:T(8,128)(2,1)S(1)}, bf16[1024,128]{1,0:T(8,128)(2,1)S(1)}, bf16[1024,128]{1,0:T(8,128)(2,1)S(1)}, bf16[1024,128]{1,0:T(8,128)(2,1)S(1)}) custom-call(s32[1]{0:T(128)} %bitcast.refs_0_.core, bf16[64,2,64,128]{3,2,1,0:T(8,128)(2,1)} %bitcast.23, f32[1,128]{1,0:T(1,128)} %bitcast.29, ...), custom_call_target="tpu_custom_call" | custom-call | flops 3221225472 | bytes 5242880 | tf_op jit(solution)/shard_map/forward/pallas_call | solution.py:155
  14.7 3.5 %collective-permute-start.4 = (bf16[1024,128]{1,0:T(8,128)(2,1)S(1)}, bf16[1024,128]{1,0:T(8,128)(2,1)S(1)}, u32[]{:S(2)}, u32[]{:S(2)}) collective-permute-start(bf16[1024,128]{1,0:T(8,128)(2,1)S(1)} %get-tuple-element.29), channel_id=1, source_target_pairs={{0,80},{1,81},{2,82},{3,83},{4,84},{5,85},{6,86},{7,87},{8,88},{9,... | collective-permute-start | bytes 786440 | tf_op jit(solution)/shard_map/ppermute | solution.py:48
  18.2 3.6 %collective-permute-start.6 = (bf16[1024,128]{1,0:T(8,128)(2,1)S(1)}, bf16[1024,128]{1,0:T(8,128)(2,1)S(1)}, u32[]{:S(2)}, u32[]{:S(2)}) collective-permute-start(bf16[1024,128]{1,0:T(8,128)(2,1)S(1)} %get-tuple-element.30), channel_id=1, source_target_pairs={{0,113},{1,112},{2,115},{3,114},{4,117},{5,116},{6,119},{7,118},{8... | collective-permute-start | bytes 786440 | tf_op jit(solution)/shard_map/ppermute | solution.py:48
  21.7 2.4 %collective-permute-start = (bf16[1024,128]{1,0:T(8,128)(2,1)S(1)}, bf16[1024,128]{1,0:T(8,128)(2,1)S(1)}, u32[]{:S(2)}, u32[]{:S(2)}) collective-permute-start(bf16[1024,128]{1,0:T(8,128)(2,1)S(1)} %get-tuple-element.27), channel_id=1, source_target_pairs={{0,33},{1,32},{2,35},{3,34},{4,37},{5,36},{6,39},{7,38},{8,41},{9,... | collective-permute-start | bytes 786440 | tf_op jit(solution)/shard_map/ppermute | solution.py:48
  24.1 3.6 %collective-permute-done.4 = bf16[1024,128]{1,0:T(8,128)(2,1)S(1)} collective-permute-done((bf16[1024,128]{1,0:T(8,128)(2,1)S(1)}, bf16[1024,128]{1,0:T(8,128)(2,1)S(1)}, u32[]{:S(2)}, u32[]{:S(2)}) %collective-permute-start.4) | collective-permute-done | bytes 262176 | tf_op jit(solution)/shard_map/ppermute | solution.py:48
  27.7 2.7 %collective-permute-start.5 = (bf16[1024,128]{1,0:T(8,128)(2,1)S(1)}, bf16[1024,128]{1,0:T(8,128)(2,1)S(1)}, u32[]{:S(2)}, u32[]{:S(2)}) collective-permute-start(bf16[1024,128]{1,0:T(8,128)(2,1)S(1)} %collective-permute-done.4), channel_id=1, source_target_pairs={{80,0},{81,16},{82,32},{83,48},{84,64},{85,80},{86,96},{87,112},{8... | collective-permute-start | bytes 786440 | tf_op jit(solution)/shard_map/ppermute | solution.py:49
  30.4 0.0 collective-permute-done.6
  30.4 2.4 %collective-permute-start.7 = (bf16[1024,128]{1,0:T(8,128)(2,1)S(1)}, bf16[1024,128]{1,0:T(8,128)(2,1)S(1)}, u32[]{:S(2)}, u32[]{:S(2)}) collective-permute-start(bf16[1024,128]{1,0:T(8,128)(2,1)S(1)} %collective-permute-done.6), channel_id=1, source_target_pairs={{113,0},{112,16},{115,32},{114,48},{117,64},{116,80},{119,96},{118... | collective-permute-start | bytes 786440 | tf_op jit(solution)/shard_map/ppermute | solution.py:49
  32.9 18.4 %all_to_all.29 = s32[8,8,128]{2,0,1:T(8,128)S(1)} all-to-all(s32[8,8,128]{2,0,1:T(8,128)S(1)} %add_bitcast_fusion), channel_id=1, replica_groups=mesh['row'=16,'col'=8] {'col'}, dimensions={1} | all-to-all | bytes 65536 | tf_op jit(solution)/shard_map/all_to_all | solution.py:404
  51.2 0.7 collective-permute-start.8
  51.9 12.5 %collective-permute-start.2 = (bf16[1024,128]{1,0:T(8,128)(2,1)S(1)}, bf16[1024,128]{1,0:T(8,128)(2,1)S(1)}, u32[]{:S(2)}, u32[]{:S(2)}) collective-permute-start(bf16[1024,128]{1,0:T(8,128)(2,1)S(1)} %get-tuple-element.28), channel_id=1, source_target_pairs={{0,8},{1,24},{2,40},{3,56},{4,72},{5,88},{6,104},{7,120},{8,0},{9,... | collective-permute-start | bytes 786440 | tf_op jit(solution)/shard_map/ppermute | solution.py:47
  64.4 0.0 collective-permute-done.8.refs_5_
  64.4 0.1 collective-permute-start.3
  64.5 0.0 collective-permute-done
  64.5 6.0 %collective-permute-start.1 = (bf16[1024,128]{1,0:T(8,128)(2,1)S(1)}, bf16[1024,128]{1,0:T(8,128)(2,1)S(1)}, u32[]{:S(2)}, u32[]{:S(2)}) collective-permute-start(bf16[1024,128]{1,0:T(8,128)(2,1)S(1)} %collective-permute-done), channel_id=1, source_target_pairs={{33,8},{32,24},{35,40},{34,56},{37,72},{36,88},{39,104},{38,120},{... | collective-permute-start | bytes 786440 | tf_op jit(solution)/shard_map/ppermute | solution.py:49
  70.5 0.0 collective-permute-done.5.refs_3_
  70.5 0.0 collective-permute-done.7.refs_4_
  70.6 13.9 %backward.2 = (f32[128,1024]{1,0:T(8,128)S(1)}, f32[128,512]{1,0:T(8,128)S(1)}, f32[256,256]{1,0:T(8,128)S(1)}, f32[24,128]{1,0:T(8,128)S(1)}) custom-call(s32[1]{0:T(128)} %bitcast.refs_0_.core, bf16[64,2,64,128]{3,2,1,0:T(8,128)(2,1)S(1)} %bitcast.24, bf16[64,2,64,128]{3,2,1,0:T(8,128)(2,1)} %get-tuple-element.26.refs_2_, ...), custom_call_target="tpu_custom_call" | custom-call | flops 4294967296 | bytes 2621440 | tf_op jit(solution)/shard_map/backward/pallas_call | solution.py:339
  84.4 0.0 collective-permute-done.3.refs_5_
  84.4 0.0 collective-permute-done.2.refs_4_
  84.4 0.0 collective-permute-done.1.refs_3_
  84.5 14.0 %backward.3 = (f32[1024,128]{1,0:T(8,128)S(1)}, f32[1024,128]{1,0:T(8,128)S(1)}) custom-call(s32[1]{0:T(128)} %bitcast.refs_0_.core, bf16[64,2,64,128]{3,2,1,0:T(8,128)(2,1)S(1)} %bitcast.25, bf16[64,2,64,128]{3,2,1,0:T(8,128)(2,1)} %get-tuple-element.26.refs_2_, bf16[1024,128]{1,0:T(8,128)(2,1)S(1)} %collective-permute-done.1.refs_3_, ...), custom_call_target="tpu_custom_call" | custom-call | flops 4294967296 | bytes 2621440 | tf_op jit(solution)/shard_map/backward/pallas_call | solution.py:339
  98.5 0.1 collective-permute-start.9
  98.6 1.9 %collective-permute-done.9 = f32[1024,128]{1,0:T(8,128)S(1)} collective-permute-done((f32[1024,128]{1,0:T(8,128)S(1)}, f32[1024,128]{1,0:T(8,128)S(1)}, u32[]{:S(2)}, u32[]{:S(2)}) %collective-permute-start.9) | collective-permute-done | bytes 524320 | tf_op jit(solution)/shard_map/ppermute | solution.py:429
  100.5 0.1 add.7
  100.5 30.5 %all_to_all.30 = f32[64,16,128]{2,1,0:T(8,128)S(1)} all-to-all(f32[64,16,128]{2,1,0:T(8,128)S(1)} %bitcast.35), channel_id=1, replica_groups={{0,1,2,3,4,5,6,7,16,17,18,19,20,21,22,23,32,33,34,35,36,37,38,39,48,49,..., dimensions={0} | all-to-all | bytes 1048576 | tf_op jit(solution)/shard_map/all_to_all | solution.py:430
  131.1 0.1 reduce_sum.9
  131.2 15.3 %all_to_all.31 = f32[64,16,128]{2,1,0:T(8,128)S(1)} all-to-all(f32[64,16,128]{2,1,0:T(8,128)S(1)} %broadcast_in_dim.2), channel_id=1, replica_groups={{0,1,2,3,4,5,6,7,16,17,18,19,20,21,22,23,32,33,34,35,36,37,38,39,48,49,..., dimensions={0} | all-to-all | bytes 1048576 | tf_op jit(solution)/shard_map/all_to_all | solution.py:434
  146.5 3.4 %collective-permute-start.10 = (f32[1024,128]{1,0:T(8,128)S(1)}, f32[1024,128]{1,0:T(8,128)S(1)}, u32[]{:S(2)}, u32[]{:S(2)}) collective-permute-start(f32[1024,128]{1,0:T(8,128)S(1)} %bitcast.17), channel_id=1, source_target_pairs={{0,8},{1,9},{2,10},{3,11},{4,12},{5,13},{6,14},{7,15},{8,0},{9,1},... | collective-permute-start | bytes 1572872 | tf_op jit(solution)/shard_map/ppermute | solution.py:442
  149.9 1.5 %collective-permute-done.10.other = f32[1024,128]{1,0:T(8,128)S(1)} collective-permute-done((f32[1024,128]{1,0:T(8,128)S(1)}, f32[1024,128]{1,0:T(8,128)S(1)}, u32[]{:S(2)}, u32[]{:S(2)}) %collective-permute-start.10) | collective-permute-done | bytes 524320 | tf_op jit(solution)/shard_map/ppermute | solution.py:442
  151.4 1.1 unpack.1
  (19 shorter events, 0.1 us)
Async XLA Ops:
  0.6 32.2 %copy-start.7 = (s32[8,1024]{1,0:T(8,128)S(1)}, s32[8,1024]{1,0:T(8,128)}, u32[]{:S(2)}) copy-start(s32[8,1024]{1,0:T(8,128)} %param.16) | copy-start | bytes 98308
  0.7 32.2 %copy-start.8 = (s32[8,1024]{1,0:T(8,128)S(1)}, s32[8,1024]{1,0:T(8,128)}, u32[]{:S(2)}) copy-start(s32[8,1024]{1,0:T(8,128)} %param.17) | copy-start | bytes 98308
  0.7 69.8 %copy-start = (bf16[64,128,128]{2,1,0:T(8,128)(2,1)S(1)}, bf16[64,128,128]{2,1,0:T(8,128)(2,1)}, u32[]{:S(2)}) copy-start(bf16[64,128,128]{2,1,0:T(8,128)(2,1)} %param.9) | copy-start | bytes 6291460
  0.7 69.8 %copy-start.1 = (bf16[128,512]{1,0:T(8,128)(2,1)S(1)}, bf16[128,512]{1,0:T(8,128)(2,1)}, u32[]{:S(2)}) copy-start(bf16[128,512]{1,0:T(8,128)(2,1)} %refs_9_.3) | copy-start | bytes 393220
  0.7 69.8 %copy-start.2 = (bf16[128,512]{1,0:T(8,128)(2,1)S(1)}, bf16[128,512]{1,0:T(8,128)(2,1)}, u32[]{:S(2)}) copy-start(bf16[128,512]{1,0:T(8,128)(2,1)} %refs_10_.3) | copy-start | bytes 393220
  0.7 69.8 %copy-start.3 = (bf16[512,128]{1,0:T(8,128)(2,1)S(1)}, bf16[512,128]{1,0:T(8,128)(2,1)}, u32[]{:S(2)}) copy-start(bf16[512,128]{1,0:T(8,128)(2,1)} %refs_11_.3) | copy-start | bytes 393220
  0.7 69.8 %copy-start.4 = (bf16[128,64]{0,1:T(8,128)(2,1)S(1)}, bf16[128,64]{0,1:T(8,128)(2,1)}, u32[]{:S(2)}) copy-start(bf16[128,64]{0,1:T(8,128)(2,1)} %param.15) | copy-start | bytes 49156
  0.7 69.8 %copy-start.5 = (f32[128]{0:T(128)S(1)}, f32[128]{0:T(128)}, u32[]{:S(2)}) copy-start(f32[128]{0:T(128)} %param.10) | copy-start | bytes 1540
  0.7 69.8 %copy-start.6 = (f32[128]{0:T(128)S(1)}, f32[128]{0:T(128)}, u32[]{:S(2)}) copy-start(f32[128]{0:T(128)} %param.11) | copy-start | bytes 1540
  14.7 13.0 %collective-permute-start.4 = (bf16[1024,128]{1,0:T(8,128)(2,1)S(1)}, bf16[1024,128]{1,0:T(8,128)(2,1)S(1)}, u32[]{:S(2)}, u32[]{:S(2)}) collective-permute-start(bf16[1024,128]{1,0:T(8,128)(2,1)S(1)} %get-tuple-element.29), channel_id=1, source_target_pairs={{0,80},{1,81},{2,82},{3,83},{4,84},{5,85},{6,86},{7,87},{8,88},{9,... | collective-permute-start | bytes 786440 | tf_op jit(solution)/shard_map/ppermute | solution.py:48
  18.2 12.2 %collective-permute-start.6 = (bf16[1024,128]{1,0:T(8,128)(2,1)S(1)}, bf16[1024,128]{1,0:T(8,128)(2,1)S(1)}, u32[]{:S(2)}, u32[]{:S(2)}) collective-permute-start(bf16[1024,128]{1,0:T(8,128)(2,1)S(1)} %get-tuple-element.30), channel_id=1, source_target_pairs={{0,113},{1,112},{2,115},{3,114},{4,117},{5,116},{6,119},{7,118},{8... | collective-permute-start | bytes 786440 | tf_op jit(solution)/shard_map/ppermute | solution.py:48
  21.7 42.7 %collective-permute-start = (bf16[1024,128]{1,0:T(8,128)(2,1)S(1)}, bf16[1024,128]{1,0:T(8,128)(2,1)S(1)}, u32[]{:S(2)}, u32[]{:S(2)}) collective-permute-start(bf16[1024,128]{1,0:T(8,128)(2,1)S(1)} %get-tuple-element.27), channel_id=1, source_target_pairs={{0,33},{1,32},{2,35},{3,34},{4,37},{5,36},{6,39},{7,38},{8,41},{9,... | collective-permute-start | bytes 786440 | tf_op jit(solution)/shard_map/ppermute | solution.py:48
  27.7 42.8 %collective-permute-start.5 = (bf16[1024,128]{1,0:T(8,128)(2,1)S(1)}, bf16[1024,128]{1,0:T(8,128)(2,1)S(1)}, u32[]{:S(2)}, u32[]{:S(2)}) collective-permute-start(bf16[1024,128]{1,0:T(8,128)(2,1)S(1)} %collective-permute-done.4), channel_id=1, source_target_pairs={{80,0},{81,16},{82,32},{83,48},{84,64},{85,80},{86,96},{87,112},{8... | collective-permute-start | bytes 786440 | tf_op jit(solution)/shard_map/ppermute | solution.py:49
  30.4 40.1 %collective-permute-start.7 = (bf16[1024,128]{1,0:T(8,128)(2,1)S(1)}, bf16[1024,128]{1,0:T(8,128)(2,1)S(1)}, u32[]{:S(2)}, u32[]{:S(2)}) collective-permute-start(bf16[1024,128]{1,0:T(8,128)(2,1)S(1)} %collective-permute-done.6), channel_id=1, source_target_pairs={{113,0},{112,16},{115,32},{114,48},{117,64},{116,80},{119,96},{118... | collective-permute-start | bytes 786440 | tf_op jit(solution)/shard_map/ppermute | solution.py:49
  51.2 13.1 %collective-permute-start.8 = (s32[64,128]{1,0:T(8,128)S(1)}, s32[64,128]{1,0:T(8,128)S(1)}, u32[]{:S(2)}, u32[]{:S(2)}) collective-permute-start(s32[64,128]{1,0:T(8,128)S(1)} %bitcast.19), channel_id=1, source_target_pairs={{0,0},{1,16},{2,32},{3,48},{4,64},{5,80},{6,96},{7,112},{8,8},{9,2... | collective-permute-start | bytes 98312 | tf_op jit(solution)/shard_map/ppermute | solution.py:47
  51.9 32.5 %collective-permute-start.2 = (bf16[1024,128]{1,0:T(8,128)(2,1)S(1)}, bf16[1024,128]{1,0:T(8,128)(2,1)S(1)}, u32[]{:S(2)}, u32[]{:S(2)}) collective-permute-start(bf16[1024,128]{1,0:T(8,128)(2,1)S(1)} %get-tuple-element.28), channel_id=1, source_target_pairs={{0,8},{1,24},{2,40},{3,56},{4,72},{5,88},{6,104},{7,120},{8,0},{9,... | collective-permute-start | bytes 786440 | tf_op jit(solution)/shard_map/ppermute | solution.py:47
  64.4 20.1 %collective-permute-start.3 = (s32[64,128]{1,0:T(8,128)S(1)}, s32[64,128]{1,0:T(8,128)S(1)}, u32[]{:S(2)}, u32[]{:S(2)}) collective-permute-start(s32[64,128]{1,0:T(8,128)S(1)} %bitcast.20), channel_id=1, source_target_pairs={{0,8},{1,24},{2,40},{3,56},{4,72},{5,88},{6,104},{7,120},{8,0},{9,... | collective-permute-start | bytes 98312 | tf_op jit(solution)/shard_map/ppermute | solution.py:47
  64.5 20.0 %collective-permute-start.1 = (bf16[1024,128]{1,0:T(8,128)(2,1)S(1)}, bf16[1024,128]{1,0:T(8,128)(2,1)S(1)}, u32[]{:S(2)}, u32[]{:S(2)}) collective-permute-start(bf16[1024,128]{1,0:T(8,128)(2,1)S(1)} %collective-permute-done), channel_id=1, source_target_pairs={{33,8},{32,24},{35,40},{34,56},{37,72},{36,88},{39,104},{38,120},{... | collective-permute-start | bytes 786440 | tf_op jit(solution)/shard_map/ppermute | solution.py:49
  98.5 2.0 %collective-permute-start.9 = (f32[1024,128]{1,0:T(8,128)S(1)}, f32[1024,128]{1,0:T(8,128)S(1)}, u32[]{:S(2)}, u32[]{:S(2)}) collective-permute-start(f32[1024,128]{1,0:T(8,128)S(1)} %get-tuple-element.36), channel_id=1, source_target_pairs={{0,8},{1,9},{2,10},{3,11},{4,12},{5,13},{6,14},{7,15},{8,0},{9,1},... | collective-permute-start | bytes 1572872 | tf_op jit(solution)/shard_map/ppermute | solution.py:429
  146.5 4.9 %collective-permute-start.10 = (f32[1024,128]{1,0:T(8,128)S(1)}, f32[1024,128]{1,0:T(8,128)S(1)}, u32[]{:S(2)}, u32[]{:S(2)}) collective-permute-start(f32[1024,128]{1,0:T(8,128)S(1)} %bitcast.17), channel_id=1, source_target_pairs={{0,8},{1,9},{2,10},{3,11},{4,12},{5,13},{6,14},{7,15},{8,0},{9,1},... | collective-permute-start | bytes 1572872 | tf_op jit(solution)/shard_map/ppermute | solution.py:442
